TPU v7x, 32 devices: a whole 2x2x4 slice. The times are simulated.
32 devices in a mesh: surf: 8 (over z, x), col: 4 (over y, core).
Axes of the slice: x: 2, y: 2, z: 4, core: 2. Of those that a mesh axis runs over, the one named last changes fastest.
Arguments:
- stiffness: float32 [32, 3, 512, 512], P(('surf', 'col'))
- load: float32 [32, 3, 512, 256], P(('surf', 'col')), may hold values from -6 to 6
- start: float32 [32, 3, 512, 256], P(('surf', 'col')), may hold values from -6 to 6
- boundary_matrix: float32 [512, 4, 2048], P('surf', None, 'col'), may hold values from -0.125 to 0.125
- bem_node: int32 [4, 512], P('col'), may hold values from 0 to 511, as said below
Outputs:
- solution_field: float32 [32, 3, 512, 256], P(('surf', 'col'))
- traction: float32 [4, 512, 256], P('col', 'surf')
Inputs may be any that keep to these rules, and one draw needn't show every extreme that they name: Each row bem_node[g] is a permutation of 0 to 512 - 1 (the top face nodes of column group g). For each block of 64 slots q in [s * 64, (s + 1) * 64) and each patch s2 of the group, the block's slots name either exactly 8 node of patch s2 or none; each patch's top face nodes lie in exactly 8 blocks.
All inputs are finite; a program needn't handle non-finite values.
Results may differ from a plain program's by a relative error of at most 0.0001.
Values sent between devices are 32-bit elements; how exact they have to be, the bound alone decides.
No kernel may reach another device: no remote copies, remote signals or barrier semaphores. Data moves between devices by JAX's collectives and lax.ppermute only.
A program may use at most 128 MiB of HBM per device.

v0:
```python
import jax
import jax.numpy as jnp
from jax import lax
from jax.sharding import PartitionSpec as P

EDGE = 8
ITERS = 2
damping = 0.25
coupling = 0.5


def with_halo(block, sides, width):
    for axis, dim in sides:
        count = lax.axis_size(axis)
        forward = [(i, i + 1) for i in range(count - 1)]
        backward = [(target, source) for source, target in forward]
        low = lax.ppermute(
            lax.slice_in_dim(block, block.shape[dim] - width, None, axis=dim), axis, forward
        )
        high = lax.ppermute(lax.slice_in_dim(block, 0, width, axis=dim), axis, backward)
        block = jnp.concatenate([low, block, high], axis=dim)
    return block


def volume_apply(current, kmats, edge_cells, layers_deep, fields):
    highest = lax.Precision.HIGHEST
    cube = current.reshape(layers_deep, edge_cells, edge_cells, edge_cells, fields)
    padded = with_halo(cube, (("surf", 1), ("col", 2)), 1)
    extra = jnp.zeros_like(cube)
    extra = extra.at[:, 0].add(cube[:, 0] - padded[:, 0, 1:-1])
    extra = extra.at[:, -1].add(cube[:, -1] - padded[:, -1, 1:-1])
    extra = extra.at[:, :, 0].add(cube[:, :, 0] - padded[:, 1:-1, 0])
    extra = extra.at[:, :, -1].add(cube[:, :, -1] - padded[:, 1:-1, -1])
    low_k = cube[:, :, :, 0]
    high_k = cube[:, :, :, -1]
    deeper = jnp.concatenate([low_k[1:], jnp.zeros_like(low_k[:1])], axis=0)
    extra = extra.at[:, :, :, -1].add(high_k - deeper)
    extra = extra.at[1:, :, :, 0].add(low_k[1:] - high_k[:-1])
    applied = jnp.einsum("dab,dbf->daf", kmats, current, precision=highest)
    return applied.reshape(cube.shape) + coupling * extra


def rank_within(labels_row, order_key):
    same_label = labels_row[:, None] == labels_row[None, :]
    earlier = order_key[None, :] < order_key[:, None]
    return jnp.sum(jnp.logical_and(same_label, earlier), axis=1)


def shards(stiffness, load, start, boundary_matrix, bem_node):
    highest = lax.Precision.HIGHEST
    surf_count = lax.axis_size("surf")
    my_index = lax.axis_index("surf")
    layers_deep = stiffness.shape[1]
    node_count = stiffness.shape[2]
    fields = load.shape[3]
    edge_cells = EDGE
    face_nodes = edge_cells * edge_cells
    per_pair = max(face_nodes // surf_count, 1)
    group_map = bem_node[0]
    group_size = group_map.shape[0]
    slot_of_node = jnp.argsort(group_map)
    kmats = stiffness[0]
    load_cube = load[0].reshape(layers_deep, edge_cells, edge_cells, edge_cells, fields)
    operator_rows = boundary_matrix.reshape(-1, group_size)
    local_order = jnp.arange(face_nodes, dtype=jnp.int32)
    my_block_nodes = lax.dynamic_slice_in_dim(group_map, my_index * face_nodes, face_nodes)
    block_owners = my_block_nodes // face_nodes
    block_local = my_block_nodes % face_nodes
    slot_index = block_owners * per_pair + rank_within(block_owners, block_local)
    my_node_slots = lax.dynamic_slice_in_dim(slot_of_node, my_index * face_nodes, face_nodes)
    node_holders = my_node_slots // face_nodes
    send_index = node_holders * per_pair + rank_within(node_holders, local_order)
    current = start[0]
    traction_rows = jnp.zeros((face_nodes, fields), jnp.float32)
    for turn_index in range(ITERS):
        cube = current.reshape(layers_deep, edge_cells, edge_cells, edge_cells, fields)
        top_face = cube[0, :, :, 0, :].reshape(face_nodes, fields)
        gathered = lax.all_gather(top_face, "surf", axis=0, tiled=True)
        ordered = jnp.take(gathered, group_map, axis=0)
        partial_value = jnp.dot(
            operator_rows, ordered, precision=highest, preferred_element_type=jnp.float32
        )
        summed = lax.psum_scatter(
            partial_value.reshape(face_nodes, -1, fields), "col", scatter_dimension=1, tiled=True
        )
        traction_rows = summed.reshape(face_nodes, fields)
        outgoing_back = (
            jnp.zeros((surf_count * per_pair, fields), jnp.float32)
            .at[slot_index]
            .set(traction_rows)
        )
        returned = lax.all_to_all(
            outgoing_back.reshape(surf_count, per_pair, fields),
            "surf",
            split_axis=0,
            concat_axis=0,
            tiled=True,
        )
        on_top = jnp.take(returned.reshape(surf_count * per_pair, fields), send_index, axis=0)
        applied = volume_apply(current, kmats, edge_cells, layers_deep, fields)
        applied = applied.at[0, :, :, 0, :].add(on_top.reshape(edge_cells, edge_cells, fields))
        residual = load_cube - applied
        current = (cube + damping * residual).reshape(layers_deep, node_count, fields)
    return (current[None], traction_rows[None])


def solution(mesh):
    in_specs = (
        P(("surf", "col"), None, None, None),
        P(("surf", "col"), None, None, None),
        P(("surf", "col"), None, None, None),
        P("surf", None, "col"),
        P("col", None),
    )
    out_specs = (P(("surf", "col"), None, None, None), P("col", "surf", None))
    return jax.shard_map(shards, mesh=mesh, in_specs=in_specs, out_specs=out_specs, check_vma=False)
```

profile of v0, /device:TPU:1, one launch (start us, length us, event | category | flops | bytes accessed | tf_op | source)
XLA Modules:
  0.0 254.0 jit_solution(10524862129218521562)
XLA Ops:
  7.2 2.1 copy.71
  11.2 4.6 %collective-permute-start = (f32[3,1,8,8,256]{4,2,1,0,3:T(8,128)}, f32[3,1,8,8,256]{4,2,1,0,3:T(8,128)}, u32[]{:S(2)}, u32[]{:S(2)}) collective-permute-start(f32[3,1,8,8,256]{4,2,1,0,3:T(8,128)} %slice.588), channel_id=1, source_target_pairs={{0,4},{4,8},{8,12},{12,16},{16,20},{20,24},{24,28},{1,5},{5,9},{9,... | collective-permute-start | bytes 589832 | tf_op jit(solution)/shard_map/ppermute | solution.py:17
  16.9 28.2 %all_gather.6 = f32[512,256]{1,0:T(8,128)} all-gather(f32[64,256]{1,0:T(8,128)S(1)} %bitcast.136), channel_id=1, replica_groups=mesh['surf'=8,'col'=4] {'surf'}, dimensions={0}, use_global_device_ids=true | all-gather | bytes 589824 | tf_op jit(solution)/shard_map/all_gather | solution.py:78
  45.2 2.0 reshape.729
  47.2 3.3 %gather_fusion = f32[512,256]{1,0:T(8,128)} fusion(f32[512,256]{1,0:T(8,128)} %all_gather.6, s32[1024]{0:T(1024)S(1)} %pad_clamp_fusion.1), kind=kCustom, calls=%fused_computation.clone | custom fusion | bytes 1050624 | tf_op jit(solution)/shard_map/jit(_take)/gather | solution.py:79
  50.5 1.9 convolution_bitcast_fusion.1
  53.2 1.7 copy.79
  54.9 5.4 %fusion.2 = f32[3,512,256]{2,1,0:T(8,128)} fusion(f32[1,3,512,512]{3,2,1,0:T(8,128)S(1)} %copy-done, f32[1,3,512,256]{3,2,1,0:T(8,128)} %param.39), kind=kOutput, calls=%fused_computation.8 | convolution fusion | flops 2415919104 | bytes 6291456 | tf_op jit(solution)/shard_map/dab,dbf->daf/dot_general | solution.py:39
  60.4 3.8 %sort.17 = (s32[512]{0:T(512)}, s32[512]{0:T(512)S(1)}) sort(s32[512]{0:T(512)S(1)} %bitcast.141, s32[512]{0:T(512)S(1)} %iota.11), dimensions={0}, to_apply=%region_3.5 | sort | flops 4608 | bytes 8192 | tf_op jit(solution)/shard_map/jit(argsort)/sort | solution.py:61
  68.8 3.3 %collective-permute-done.1 = f32[3,1,8,8,256]{4,2,1,0,3:T(8,128)S(1)} collective-permute-done((f32[3,1,8,8,256]{4,2,1,0,3:T(8,128)S(1)}, f32[3,1,8,8,256]{4,2,1,0,3:T(8,128)S(1)}, u32[]{:S(2)}, u32[]{:S(2)}) %collective-permute-start.1) | collective-permute-done | bytes 196640 | tf_op jit(solution)/shard_map/ppermute | solution.py:20
  74.9 10.4 %collective-permute-start.2 = (f32[3,10,1,8,256]{4,2,1,0,3:T(1,128)}, f32[3,10,1,8,256]{4,2,1,0,3:T(1,128)}, u32[]{:S(2)}, u32[]{:S(2)}) collective-permute-start(f32[3,10,1,8,256]{4,2,1,0,3:T(1,128)} %get-tuple-element.181), channel_id=1, source_target_pairs={{0,1},{1,2},{2,3},{4,5},{5,6},{6,7},{8,9},{9,10},{10,11},{12,13},{... | collective-permute-start | bytes 737288 | tf_op jit(solution)/shard_map/ppermute | solution.py:17
  85.5 1.9 collective-permute-start.3
  87.4 1.7 scatter_custom_fusion
  89.1 3.4 %all-to-all-start = ((f32[8,8,256]{2,1,0:T(8,128)}), f32[8,8,256]{2,1,0:T(8,128)S(1)}, u32[]{:S(2)}, u32[]{:S(2)}) async-start(f32[8,8,256]{2,1,0:T(8,128)} %bitcast.16), calls=%async_computation.1 | async-start | bytes 131072 | tf_op jit(solution)/shard_map/all_to_all | solution.py:92
  92.7 2.3 fusion.25
  95.0 4.5 %scatter-add.50 = f32[3,8,8,8,256]{4,2,1,0,3:T(8,128)} dynamic-update-slice(f32[3,8,8,8,256]{4,2,1,0,3:T(8,128)} %get-tuple-element.193, f32[3,8,1,8,256]{4,2,1,0,3:T(1,128)S(1)} %fusion.25, s32[]{:T(128)} %constant.397.clone.1, s32[]{:T(128)} %constant.397.clone.1, s32[]{:T(128)} %constant.397.clone.1, s32[]{:T(128)} %constant.397.clone.1, s32[]{:T(128)} %constant.397.clone.1) | dynamic-update-slice | bytes 393220 | tf_op jit(solution)/shard_map/scatter-add | solution.py:32
  99.5 2.4 fusion.24
  101.9 4.5 %scatter-add.51 = f32[3,8,8,8,256]{4,2,1,0,3:T(8,128)} dynamic-update-slice(f32[3,8,8,8,256]{4,2,1,0,3:T(8,128)} %scatter-add.50, f32[3,8,1,8,256]{4,2,1,0,3:T(1,128)S(1)} %fusion.24, s32[]{:T(128)} %constant.397.clone.1, s32[]{:T(128)} %constant.397.clone.1, s32[]{:T(128)} %constant.398.clone.1, s32[]{:T(128)} %constant.397.clone.1, s32[]{:T(128)} %constant.397.clone.1) | dynamic-update-slice | bytes 393220 | tf_op jit(solution)/shard_map/scatter-add | solution.py:33
  106.4 1.7 fusion.23
  108.1 3.5 %copy.78 = f32[3,8,8,8,256]{4,3,2,1,0:T(8,128)} copy(f32[3,8,8,8,256]{4,2,1,0,3:T(8,128)} %fusion.23) | data formatting | bytes 3145728 | tf_op jit(solution)/shard_map/scatter-add | solution.py:37
  112.5 1.8 fusion.27
  114.3 4.0 %scatter-add.55 = f32[3,8,8,8,256]{4,3,2,1,0:T(8,128)} dynamic-update-slice(f32[3,8,8,8,256]{4,3,2,1,0:T(8,128)} %copy.78, f32[2,8,8,1,256]{4,3,2,1,0:T(1,128)S(1)} %fusion.27, s32[]{:T(128)} %constant.399.clone.1, s32[]{:T(128)} %constant.397.clone.1, s32[]{:T(128)} %constant.397.clone.1, s32[]{:T(128)} %constant.397.clone.1, s32[]{:T(128)} %constant.397.clone.1) | dynamic-update-slice | bytes 262148 | tf_op jit(solution)/shard_map/scatter-add | solution.py:38
  118.3 3.3 %multiply_add_fusion.3 = f32[3,8,8,8,256]{4,3,2,1,0:T(8,128)} fusion(f32[3,8,8,8,256]{4,3,2,1,0:T(8,128)} %bitcast.130, f32[3,8,8,8,256]{4,3,2,1,0:T(8,128)} %scatter-add.55), kind=kLoop, calls=%fused_computation.14 | loop fusion | flops 786432 | bytes 4718592 | tf_op jit(solution)/shard_map/add | solution.py:40
  123.5 2.3 scatter-add.56
  125.8 2.8 %multiply_add_fusion.2 = f32[3,8,8,8,256]{4,3,2,1,0:T(8,128)S(1)} fusion(f32[3,8,8,8,256]{4,3,2,1,0:T(8,128)} %bitcast.124, f32[3,8,8,8,256]{4,3,2,1,0:T(8,128)} %bitcast.128, f32[3,8,8,8,256]{4,3,2,1,0:T(8,128)} %scatter-add.56), kind=kLoop, calls=%fused_computation.13 | loop fusion | flops 1179648 | bytes 6291456 | tf_op jit(solution)/shard_map/add | solution.py:103
  131.6 3.7 %collective-permute-start.4 = (f32[3,1,8,8,256]{4,2,1,0,3:T(8,128)}, f32[3,1,8,8,256]{4,2,1,0,3:T(8,128)}, u32[]{:S(2)}, u32[]{:S(2)}) collective-permute-start(f32[3,1,8,8,256]{4,2,1,0,3:T(8,128)} %slice.605), channel_id=1, source_target_pairs={{0,4},{4,8},{8,12},{12,16},{16,20},{20,24},{24,28},{1,5},{5,9},{9,... | collective-permute-start | bytes 589832 | tf_op jit(solution)/shard_map/ppermute | solution.py:17
  135.3 28.4 %all_gather.7 = f32[512,256]{1,0:T(8,128)} all-gather(f32[64,256]{1,0:T(8,128)S(1)} %bitcast.137), channel_id=1, replica_groups=mesh['surf'=8,'col'=4] {'surf'}, dimensions={0}, use_global_device_ids=true | all-gather | bytes 589824 | tf_op jit(solution)/shard_map/all_gather | solution.py:78
  163.7 3.3 %gather_fusion.2 = f32[512,256]{1,0:T(8,128)} fusion(f32[512,256]{1,0:T(8,128)} %all_gather.7, s32[1024]{0:T(1024)S(1)} %pad_clamp_fusion.1), kind=kCustom, calls=%fused_computation.2.clone | custom fusion | bytes 1050624 | tf_op jit(solution)/shard_map/jit(_take)/gather | solution.py:79
  167.0 1.9 convolution_bitcast_fusion
  175.8 4.6 %collective-permute-done.5 = f32[3,1,8,8,256]{4,2,1,0,3:T(8,128)S(1)} collective-permute-done((f32[3,1,8,8,256]{4,2,1,0,3:T(8,128)S(1)}, f32[3,1,8,8,256]{4,2,1,0,3:T(8,128)S(1)}, u32[]{:S(2)}, u32[]{:S(2)}) %collective-permute-start.5) | collective-permute-done | bytes 196640 | tf_op jit(solution)/shard_map/ppermute | solution.py:20
  180.4 1.7 constant_dynamic-update-slice_fusion.3
  183.2 10.5 %collective-permute-start.6 = (f32[3,10,1,8,256]{4,2,1,0,3:T(1,128)}, f32[3,10,1,8,256]{4,2,1,0,3:T(1,128)}, u32[]{:S(2)}, u32[]{:S(2)}) collective-permute-start(f32[3,10,1,8,256]{4,2,1,0,3:T(1,128)} %get-tuple-element.179), channel_id=1, source_target_pairs={{0,1},{1,2},{2,3},{4,5},{5,6},{6,7},{8,9},{9,10},{10,11},{12,13},{... | collective-permute-start | bytes 737288 | tf_op jit(solution)/shard_map/ppermute | solution.py:17
  193.7 6.5 %fusion.5 = f32[3,512,256]{1,2,0:T(8,128)} fusion(f32[3,512,256]{2,1,0:T(8,128)S(1)} %bitcast.120, f32[1,3,512,512]{3,2,1,0:T(8,128)S(1)} %copy-done), kind=kOutput, calls=%fused_computation.15 | convolution fusion | flops 2415919104 | bytes 6291456 | tf_op jit(solution)/shard_map/dab,dbf->daf/dot_general | solution.py:39
  200.3 3.0 %copy.82 = f32[3,512,256]{2,1,0:T(8,128)} copy(f32[3,512,256]{1,2,0:T(8,128)} %fusion.5) | data formatting | bytes 3145728 | tf_op jit(solution)/shard_map/dab,dbf->daf/dot_general | solution.py:39
  203.3 1.8 fusion.42
  205.1 1.9 collective-permute-start.7
  208.8 3.3 %all-to-all-start.1 = ((f32[8,8,256]{2,1,0:T(8,128)}), f32[8,8,256]{2,1,0:T(8,128)S(1)}, u32[]{:S(2)}, u32[]{:S(2)}) async-start(f32[8,8,256]{2,1,0:T(8,128)} %bitcast.26), calls=%async_computation.3 | async-start | bytes 131072 | tf_op jit(solution)/shard_map/all_to_all | solution.py:92
  212.1 1.8 fusion.19
  214.0 4.5 %scatter-add.61 = f32[3,8,8,8,256]{4,2,1,0,3:T(8,128)} dynamic-update-slice(f32[3,8,8,8,256]{4,2,1,0,3:T(8,128)} %get-tuple-element.191, f32[3,8,1,8,256]{4,2,1,0,3:T(1,128)S(1)} %fusion.19, s32[]{:T(128)} %constant.397.clone.1, s32[]{:T(128)} %constant.397.clone.1, s32[]{:T(128)} %constant.397.clone.1, s32[]{:T(128)} %constant.397.clone.1, s32[]{:T(128)} %constant.397.clone.1) | dynamic-update-slice | bytes 393220 | tf_op jit(solution)/shard_map/scatter-add | solution.py:32
  218.5 1.9 fusion.18
  220.4 4.5 %scatter-add.64 = f32[3,8,8,8,256]{4,2,1,0,3:T(8,128)} dynamic-update-slice(f32[3,8,8,8,256]{4,2,1,0,3:T(8,128)} %scatter-add.61, f32[3,8,1,8,256]{4,2,1,0,3:T(1,128)S(1)} %fusion.18, s32[]{:T(128)} %constant.397.clone.1, s32[]{:T(128)} %constant.397.clone.1, s32[]{:T(128)} %constant.398.clone.1, s32[]{:T(128)} %constant.397.clone.1, s32[]{:T(128)} %constant.397.clone.1) | dynamic-update-slice | bytes 393220 | tf_op jit(solution)/shard_map/scatter-add | solution.py:33
  224.9 1.7 fusion.17
  227.5 1.8 fusion.26
  229.3 3.5 %copy.90 = f32[3,8,8,8,256]{4,3,2,1,0:T(8,128)} copy(f32[3,8,8,8,256]{4,2,1,0,3:T(8,128)} %fusion.17) | data formatting | bytes 3145728 | tf_op jit(solution)/shard_map/scatter-add | solution.py:37
  233.5 4.0 %scatter-add.66 = f32[3,8,8,8,256]{4,3,2,1,0:T(8,128)} dynamic-update-slice(f32[3,8,8,8,256]{4,3,2,1,0:T(8,128)} %copy.90, f32[2,8,8,1,256]{4,3,2,1,0:T(1,128)S(1)} %fusion.26, s32[]{:T(128)} %constant.399.clone.1, s32[]{:T(128)} %constant.397.clone.1, s32[]{:T(128)} %constant.397.clone.1, s32[]{:T(128)} %constant.397.clone.1, s32[]{:T(128)} %constant.397.clone.1) | dynamic-update-slice | bytes 262148 | tf_op jit(solution)/shard_map/scatter-add | solution.py:38
  237.5 2.1 multiply_add_fusion.1
  240.9 2.3 scatter-add.69
  243.2 3.9 %multiply_add_fusion = f32[3,8,8,8,256]{4,3,2,1,0:T(8,128)} fusion(f32[3,8,8,8,256]{4,3,2,1,0:T(8,128)} %copy-done.1, f32[3,8,8,8,256]{4,3,2,1,0:T(8,128)} %bitcast.129, f32[3,8,8,8,256]{4,3,2,1,0:T(8,128)} %scatter-add.69), kind=kLoop, calls=%fused_computation.11 | loop fusion | flops 1179648 | bytes 6291456 | tf_op jit(solution)/shard_map/add | solution.py:103
  (78 shorter events, 30.0 us)
Async XLA Ops:
  7.2 47.8 %copy-start = (f32[1,3,512,512]{3,2,1,0:T(8,128)S(1)}, f32[1,3,512,512]{3,2,1,0:T(8,128)}, u32[]{:S(2)}) copy-start(f32[1,3,512,512]{3,2,1,0:T(8,128)} %param.37) | copy-start | bytes 9437188
  7.2 80.2 %reduce-scatter.3.cloned.1.call-start = ((), (), s32[]{:S(2)}) async-start(), calls=%async_computation.4 | async-start | bytes 327680 | tf_op jit(solution)/shard_map/reduce_scatter | solution.py:83
  7.2 9.6 %copy-start.7 = (s32[1,512]{1,0:T(1,128)S(1)}, s32[1,512]{1,0:T(1,128)}, u32[]{:S(2)}) copy-start(s32[1,512]{1,0:T(1,128)} %param.41) | copy-start | bytes 6148
  9.3 1.2 copy-start.5
  11.2 53.5 %collective-permute-start = (f32[3,1,8,8,256]{4,2,1,0,3:T(8,128)}, f32[3,1,8,8,256]{4,2,1,0,3:T(8,128)}, u32[]{:S(2)}, u32[]{:S(2)}) collective-permute-start(f32[3,1,8,8,256]{4,2,1,0,3:T(8,128)} %slice.588), channel_id=1, source_target_pairs={{0,4},{4,8},{8,12},{12,16},{16,20},{20,24},{24,28},{1,5},{5,9},{9,... | collective-permute-start | bytes 589832 | tf_op jit(solution)/shard_map/ppermute | solution.py:17
  64.2 4.2 %copy-start.3 = (f32[1,3,512,256]{3,2,1,0:T(8,128)S(1)}, f32[1,3,512,256]{3,2,1,0:T(8,128)}, u32[]{:S(2)}) copy-start(f32[1,3,512,256]{3,2,1,0:T(8,128)} %param.39) | copy-start | bytes 4718596
  65.8 6.4 %collective-permute-start.1 = (f32[3,1,8,8,256]{4,2,1,0,3:T(8,128)S(1)}, f32[3,1,8,8,256]{4,2,1,0,3:T(8,128)S(1)}, u32[]{:S(2)}, u32[]{:S(2)}) collective-permute-start(f32[3,1,8,8,256]{4,2,1,0,3:T(8,128)S(1)} %get-tuple-element.186), channel_id=1, source_target_pairs={{4,0},{8,4},{12,8},{16,12},{20,16},{24,20},{28,24},{5,1},{9,5},{13... | collective-permute-start | bytes 589832 | tf_op jit(solution)/shard_map/ppermute | solution.py:20
  74.9 17.8 %collective-permute-start.2 = (f32[3,10,1,8,256]{4,2,1,0,3:T(1,128)}, f32[3,10,1,8,256]{4,2,1,0,3:T(1,128)}, u32[]{:S(2)}, u32[]{:S(2)}) collective-permute-start(f32[3,10,1,8,256]{4,2,1,0,3:T(1,128)} %get-tuple-element.181), channel_id=1, source_target_pairs={{0,1},{1,2},{2,3},{4,5},{5,6},{6,7},{8,9},{9,10},{10,11},{12,13},{... | collective-permute-start | bytes 737288 | tf_op jit(solution)/shard_map/ppermute | solution.py:17
  85.5 3.7 %copy-start.8 = (s32[64]{0:T(128)}, s32[64]{0:T(128)S(1)}, u32[]{:S(2)}) copy-start(s32[64]{0:T(128)S(1)} %fusion.36) | copy-start | bytes 772
  85.5 14.0 %collective-permute-start.3 = (f32[3,10,1,8,256]{4,2,1,0,3:T(1,128)}, f32[3,10,1,8,256]{4,2,1,0,3:T(1,128)}, u32[]{:S(2)}, u32[]{:S(2)}) collective-permute-start(f32[3,10,1,8,256]{4,2,1,0,3:T(1,128)} %get-tuple-element.180), channel_id=1, source_target_pairs={{1,0},{2,1},{3,2},{5,4},{6,5},{7,6},{9,8},{10,9},{11,10},{13,12},{... | collective-permute-start | bytes 737288 | tf_op jit(solution)/shard_map/ppermute | solution.py:20
  89.1 32.5 %all-to-all-start = ((f32[8,8,256]{2,1,0:T(8,128)}), f32[8,8,256]{2,1,0:T(8,128)S(1)}, u32[]{:S(2)}, u32[]{:S(2)}) async-start(f32[8,8,256]{2,1,0:T(8,128)} %bitcast.16), calls=%async_computation.1 | async-start | bytes 131072 | tf_op jit(solution)/shard_map/all_to_all | solution.py:92
  92.5 114.6 %reduce-scatter.5.cloned.1.call-start = ((), (), s32[]{:S(2)}) async-start(), calls=%async_computation.5 | async-start | bytes 327680 | tf_op jit(solution)/shard_map/reduce_scatter | solution.py:83
  128.6 1.1 copy-start.1
  129.7 1.2 copy-start.6
  131.6 39.9 %collective-permute-start.4 = (f32[3,1,8,8,256]{4,2,1,0,3:T(8,128)}, f32[3,1,8,8,256]{4,2,1,0,3:T(8,128)}, u32[]{:S(2)}, u32[]{:S(2)}) collective-permute-start(f32[3,1,8,8,256]{4,2,1,0,3:T(8,128)} %slice.605), channel_id=1, source_target_pairs={{0,4},{4,8},{8,12},{12,16},{16,20},{20,24},{24,28},{1,5},{5,9},{9,... | collective-permute-start | bytes 589832 | tf_op jit(solution)/shard_map/ppermute | solution.py:17
  171.4 3.9 %copy-start.2 = (f32[3,8,8,8,256]{4,3,2,1,0:T(8,128)S(1)}, f32[3,8,8,8,256]{4,3,2,1,0:T(8,128)}, u32[]{:S(2)}) copy-start(f32[3,8,8,8,256]{4,3,2,1,0:T(8,128)} %copy-done.1) | copy-start | bytes 4718596
  174.0 6.4 %collective-permute-start.5 = (f32[3,1,8,8,256]{4,2,1,0,3:T(8,128)S(1)}, f32[3,1,8,8,256]{4,2,1,0,3:T(8,128)S(1)}, u32[]{:S(2)}, u32[]{:S(2)}) collective-permute-start(f32[3,1,8,8,256]{4,2,1,0,3:T(8,128)S(1)} %get-tuple-element.184), channel_id=1, source_target_pairs={{4,0},{8,4},{12,8},{16,12},{20,16},{24,20},{28,24},{5,1},{9,5},{13... | collective-permute-start | bytes 589832 | tf_op jit(solution)/shard_map/ppermute | solution.py:20
  183.2 28.9 %collective-permute-start.6 = (f32[3,10,1,8,256]{4,2,1,0,3:T(1,128)}, f32[3,10,1,8,256]{4,2,1,0,3:T(1,128)}, u32[]{:S(2)}, u32[]{:S(2)}) collective-permute-start(f32[3,10,1,8,256]{4,2,1,0,3:T(1,128)} %get-tuple-element.179), channel_id=1, source_target_pairs={{0,1},{1,2},{2,3},{4,5},{5,6},{6,7},{8,9},{9,10},{10,11},{12,13},{... | collective-permute-start | bytes 737288 | tf_op jit(solution)/shard_map/ppermute | solution.py:17
  205.1 13.3 %collective-permute-start.7 = (f32[3,10,1,8,256]{4,2,1,0,3:T(1,128)}, f32[3,10,1,8,256]{4,2,1,0,3:T(1,128)}, u32[]{:S(2)}, u32[]{:S(2)}) collective-permute-start(f32[3,10,1,8,256]{4,2,1,0,3:T(1,128)} %get-tuple-element.178), channel_id=1, source_target_pairs={{1,0},{2,1},{3,2},{5,4},{6,5},{7,6},{9,8},{10,9},{11,10},{13,12},{... | collective-permute-start | bytes 737288 | tf_op jit(solution)/shard_map/ppermute | solution.py:20
  208.8 24.0 %all-to-all-start.1 = ((f32[8,8,256]{2,1,0:T(8,128)}), f32[8,8,256]{2,1,0:T(8,128)S(1)}, u32[]{:S(2)}, u32[]{:S(2)}) async-start(f32[8,8,256]{2,1,0:T(8,128)} %bitcast.26), calls=%async_computation.3 | async-start | bytes 131072 | tf_op jit(solution)/shard_map/all_to_all | solution.py:92
  239.6 1.2 copy-start.4
Sparse Core Ops, SparseCore 0:
  55.0 24.3 reduce-scatter.2
  171.5 24.3 reduce-scatter.4
where the time goes:
time: 256 us; the launch traced here: 254 us
  local copies, waits for them, and re-layouts  77.7 us (30%)
  blocking collectives  56.6 us (22%)
  starting transfers between devices  42.6 us (17%)
  other arithmetic  38.9 us (15%)
  matrix products  15.7 us (6%)
  between operations  14.4 us (6%)
  waiting for transfers between devices  8.06 us (3%)
    all_gather x2, blocking collectives, shards(): gathered = lax.all_gather(top_face, 'surf', axis=0, tiled=True)  56.6 us
    ppermute x4, starting transfers between devices, with_halo(): lax.ppermute(lax.slice_in_dim(block, block.shape[dim] - width, None, axis...  29.2 us
    dot_general x2, matrix products, volume_apply(): applied = jnp.einsum('dab,dbf->daf', kmats, current, precision=highest)  11.9 us
    scatter-add x2, local copies, waits for them, and re-layouts, volume_apply(): extra = extra.at[:, :, 0].add(cube[:, :, 0] - padded[:, 1:-1, 0])  8.99 us
    scatter-add x2, local copies, waits for them, and re-layouts, volume_apply(): extra = extra.at[:, :, -1].add(cube[:, :, -1] - padded[:, 1:-1, -1])  8.99 us
    scatter-add x2, local copies, waits for them, and re-layouts, volume_apply(): extra = extra.at[1:, :, :, 0].add(low_k[1:] - high_k[:-1])  8 us
    ppermute x4, waiting for transfers between devices, with_halo(): lax.ppermute(lax.slice_in_dim(block, 0, width, axis=dim), axis, backward)  7.97 us
    scatter-add x2, local copies, waits for them, and re-layouts, volume_apply(): extra = extra.at[:, :, :, -1].add(high_k - deeper)  6.98 us
  transfers between devices with their start and end apart: 12, of which 2 were waited for; matrix products, arithmetic and copies ran while one was open for 41% of the time, Pallas kernels for 0%

commit v1 on v0

--- a/solution.py
+++ b/solution.py
@@ -75,7 +75,14 @@
     for turn_index in range(ITERS):
         cube = current.reshape(layers_deep, edge_cells, edge_cells, edge_cells, fields)
         top_face = cube[0, :, :, 0, :].reshape(face_nodes, fields)
-        gathered = lax.all_gather(top_face, "surf", axis=0, tiled=True)
+        n_dev = lax.axis_size("surf")
+        right = [(i_2, (i_2 + 1) % n_dev) for i_2 in range(n_dev)]
+        pieces = [top_face]
+        for stride in range(1, n_dev):
+            pieces = [lax.ppermute(pieces[0], "surf", right), *pieces]
+        full = jnp.concatenate(pieces, axis=0)
+        turn = (lax.axis_index("surf") + 1) * pieces[-1].shape[0]
+        gathered = jnp.roll(full, turn, axis=0)
         ordered = jnp.take(gathered, group_map, axis=0)
         partial_value = jnp.dot(
             operator_rows, ordered, precision=highest, preferred_element_type=jnp.float32

time: 256 us -> 242 us (0.945)
  blocking collectives: 56.6 us -> 0 us
  waiting for transfers between devices: 8.06 us -> 35 us
  starting transfers between devices: 42.6 us -> 51.1 us
  other arithmetic: 38.9 us -> 44.8 us
    all_gather x2 -> x0, blocking collectives: 56.6 us -> none  [shards(): gathered = lax.all_gather(top_face, 'surf', axis=0, tiled=True)]
    ppermute x0 -> x14, waiting for transfers between devices: none -> 30.1 us  [shards(): pieces = [lax.ppermute(pieces[0], 'surf', right), *pieces]]
    ppermute x4, waiting for transfers between devices: 7.97 us -> 0.01 us  [with_halo(): lax.ppermute(lax.slice_in_dim(block, 0, width, axis=dim), axis, backward)]
    all_to_all x2, waiting for transfers between devices: 0.01 us -> 4.85 us  [shards(): lax.all_to_all(outgoing_back.reshape(surf_count, per_pair, fields), 'surf...]
    all_to_all x2, starting transfers between devices: 6.7 us -> 11.4 us  [shards(): lax.all_to_all(outgoing_back.reshape(surf_count, per_pair, fields), 'surf...]
    unnamed x24 -> x38, local copies, waits for them, and re-layouts: 5.05 us -> 8.53 us
    ppermute x0 -> x14, starting transfers between devices: none -> 3.17 us  [shards(): pieces = [lax.ppermute(pieces[0], 'surf', right), *pieces]]
  transfers between devices with their start and end apart: 12 -> 26, of which waited for: 2 -> 12; matrix products, arithmetic and copies ran while one was open for 41% -> 48% of each run, Pallas kernels for 0% -> 0%
where the time goes in v1:
time: 242 us; the launch traced here: 239 us
  local copies, waits for them, and re-layouts  79.6 us (33%)
  starting transfers between devices  51.1 us (21%)
  other arithmetic  44.8 us (19%)
  waiting for transfers between devices  35 us (14%)
  between operations  14.5 us (6%)
  matrix products  14.3 us (6%)
    ppermute x14, waiting for transfers between devices, shards(): pieces = [lax.ppermute(pieces[0], 'surf', right), *pieces]  30.1 us
    ppermute x4, starting transfers between devices, with_halo(): lax.ppermute(lax.slice_in_dim(block, block.shape[dim] - width, None, axis...  29.6 us
    all_to_all x2, starting transfers between devices, shards(): lax.all_to_all(outgoing_back.reshape(surf_count, per_pair, fields), 'surf...  11.4 us
    dot_general x2, matrix products, volume_apply(): applied = jnp.einsum('dab,dbf->daf', kmats, current, precision=highest)  10.5 us
    scatter-add x2, local copies, waits for them, and re-layouts, volume_apply(): extra = extra.at[:, :, -1].add(cube[:, :, -1] - padded[:, 1:-1, -1])  9 us
    scatter-add x2, local copies, waits for them, and re-layouts, volume_apply(): extra = extra.at[:, :, 0].add(cube[:, :, 0] - padded[:, 1:-1, 0])  8.99 us
    unnamed x38, local copies, waits for them, and re-layouts  8.53 us
    scatter-add x2, local copies, waits for them, and re-layouts, volume_apply(): extra = extra.at[1:, :, :, 0].add(low_k[1:] - high_k[:-1])  7.98 us
  transfers between devices with their start and end apart: 26, of which 12 were waited for; matrix products, arithmetic and copies ran while one was open for 48% of the time, Pallas kernels for 0%

profile of v1, /device:TPU:1, one launch (start us, length us, event | category | flops | bytes accessed | tf_op | source)
XLA Modules:
  0.0 239.3 jit_solution(15394127891354084897)
XLA Ops:
  7.2 2.1 copy.71
  11.2 4.6 %collective-permute-start = (f32[3,1,8,8,256]{4,2,1,0,3:T(8,128)}, f32[3,1,8,8,256]{4,2,1,0,3:T(8,128)}, u32[]{:S(2)}, u32[]{:S(2)}) collective-permute-start(f32[3,1,8,8,256]{4,2,1,0,3:T(8,128)} %slice.588), channel_id=1, source_target_pairs={{0,4},{4,8},{8,12},{12,16},{16,20},{20,24},{24,28},{1,5},{5,9},{9,... | collective-permute-start | bytes 589832 | tf_op jit(solution)/shard_map/ppermute | solution.py:17
  16.5 4.0 %fusion.2 = f32[3,512,256]{2,1,0:T(8,128)} fusion(f32[1,3,512,512]{3,2,1,0:T(8,128)S(1)} %copy-done, f32[1,3,512,256]{3,2,1,0:T(8,128)S(1)} %copy-done.2), kind=kOutput, calls=%fused_computation.8 | convolution fusion | flops 2415919104 | bytes 6291456 | tf_op jit(solution)/shard_map/dab,dbf->daf/dot_general | solution.py:39
  20.6 3.8 %sort.17 = (s32[512]{0:T(512)}, s32[512]{0:T(512)S(1)}) sort(s32[512]{0:T(512)S(1)} %bitcast.145, s32[512]{0:T(512)S(1)} %iota.11), dimensions={0}, to_apply=%region_3.6 | sort | flops 4608 | bytes 8192 | tf_op jit(solution)/shard_map/jit(argsort)/sort | solution.py:61
  28.5 2.0 reshape.729
  31.8 5.5 %collective-permute-done.6 = f32[64,256]{1,0:T(8,128)S(1)} collective-permute-done((f32[64,256]{1,0:T(8,128)}, f32[64,256]{1,0:T(8,128)S(1)}, u32[]{:S(2)}, u32[]{:S(2)}) %collective-permute-start.6) | collective-permute-done | bytes 65568 | tf_op jit(solution)/shard_map/ppermute | solution.py:82
  37.9 5.2 %collective-permute-done.7 = f32[64,256]{1,0:T(8,128)S(1)} collective-permute-done((f32[64,256]{1,0:T(8,128)S(1)}, f32[64,256]{1,0:T(8,128)S(1)}, u32[]{:S(2)}, u32[]{:S(2)}) %collective-permute-start.7) | collective-permute-done | bytes 65568 | tf_op jit(solution)/shard_map/ppermute | solution.py:82
  45.5 3.5 %collective-permute-done.8 = f32[64,256]{1,0:T(8,128)S(1)} collective-permute-done((f32[64,256]{1,0:T(8,128)S(1)}, f32[64,256]{1,0:T(8,128)S(1)}, u32[]{:S(2)}, u32[]{:S(2)}) %collective-permute-start.8) | collective-permute-done | bytes 65568 | tf_op jit(solution)/shard_map/ppermute | solution.py:82
  49.0 1.9 constant_dynamic-update-slice_fusion.1
  52.2 2.7 %collective-permute-done.9 = f32[64,256]{1,0:T(8,128)S(1)} collective-permute-done((f32[64,256]{1,0:T(8,128)S(1)}, f32[64,256]{1,0:T(8,128)S(1)}, u32[]{:S(2)}, u32[]{:S(2)}) %collective-permute-start.9) | collective-permute-done | bytes 65568 | tf_op jit(solution)/shard_map/ppermute | solution.py:82
  57.7 10.2 %collective-permute-start.2 = (f32[3,10,1,8,256]{4,2,1,0,3:T(1,128)}, f32[3,10,1,8,256]{4,2,1,0,3:T(1,128)}, u32[]{:S(2)}, u32[]{:S(2)}) collective-permute-start(f32[3,10,1,8,256]{4,2,1,0,3:T(1,128)} %get-tuple-element.182), channel_id=1, source_target_pairs={{0,1},{1,2},{2,3},{4,5},{5,6},{6,7},{8,9},{9,10},{10,11},{12,13},{... | collective-permute-start | bytes 737288 | tf_op jit(solution)/shard_map/ppermute | solution.py:17
  67.9 2.1 collective-permute-start.3
  72.0 3.3 %gather_fusion = f32[512,256]{1,0:T(8,128)} fusion(f32[512,256]{1,0:T(8,128)} %fusion.9, s32[1024]{0:T(1024)S(1)} %pad_clamp_fusion.1), kind=kCustom, calls=%fused_computation.clone | custom fusion | bytes 1050624 | tf_op jit(solution)/shard_map/jit(_take)/gather | solution.py:86
  75.3 1.9 convolution_bitcast_fusion.1
  79.7 2.3 fusion.27
  82.0 4.5 %scatter-add.50 = f32[3,8,8,8,256]{4,2,1,0,3:T(8,128)} dynamic-update-slice(f32[3,8,8,8,256]{4,2,1,0,3:T(8,128)} %get-tuple-element.194, f32[3,8,1,8,256]{4,2,1,0,3:T(1,128)S(1)} %fusion.27, s32[]{:T(128)} %constant.415.clone.1, s32[]{:T(128)} %constant.415.clone.1, s32[]{:T(128)} %constant.415.clone.1, s32[]{:T(128)} %constant.415.clone.1, s32[]{:T(128)} %constant.415.clone.1) | dynamic-update-slice | bytes 393220 | tf_op jit(solution)/shard_map/scatter-add | solution.py:32
  86.5 2.4 %fusion.26 = f32[3,8,1,8,256]{4,2,1,0,3:T(1,128)S(1)} fusion(f32[3,10,1,8,256]{4,2,1,0,3:T(1,128)} %collective-permute-done.3, f32[3,8,8,8,256]{4,2,1,0,3:T(8,128)} %copy-done.3, f32[3,8,8,8,256]{4,2,1,0,3:T(8,128)} %scatter-add.50), kind=kLoop, calls=%fused_computation.45 | loop fusion | flops 98304 | bytes 786432 | tf_op jit(solution)/shard_map/add | solution.py:33
  88.9 4.5 %scatter-add.51 = f32[3,8,8,8,256]{4,2,1,0,3:T(8,128)} dynamic-update-slice(f32[3,8,8,8,256]{4,2,1,0,3:T(8,128)} %scatter-add.50, f32[3,8,1,8,256]{4,2,1,0,3:T(1,128)S(1)} %fusion.26, s32[]{:T(128)} %constant.415.clone.1, s32[]{:T(128)} %constant.415.clone.1, s32[]{:T(128)} %constant.416.clone.1, s32[]{:T(128)} %constant.415.clone.1, s32[]{:T(128)} %constant.415.clone.1) | dynamic-update-slice | bytes 393220 | tf_op jit(solution)/shard_map/scatter-add | solution.py:33
  95.1 3.5 %copy.78 = f32[3,8,8,8,256]{4,3,2,1,0:T(8,128)} copy(f32[3,8,8,8,256]{4,2,1,0,3:T(8,128)} %fusion.25) | data formatting | bytes 3145728 | tf_op jit(solution)/shard_map/scatter-add | solution.py:37
  101.4 4.0 %scatter-add.55 = f32[3,8,8,8,256]{4,3,2,1,0:T(8,128)} dynamic-update-slice(f32[3,8,8,8,256]{4,3,2,1,0:T(8,128)} %copy.78, f32[2,8,8,1,256]{4,3,2,1,0:T(1,128)S(1)} %fusion.29, s32[]{:T(128)} %constant.417.clone.1, s32[]{:T(128)} %constant.415.clone.1, s32[]{:T(128)} %constant.415.clone.1, s32[]{:T(128)} %constant.415.clone.1, s32[]{:T(128)} %constant.415.clone.1) | dynamic-update-slice | bytes 262148 | tf_op jit(solution)/shard_map/scatter-add | solution.py:38
  107.0 5.7 %all-to-all-start = ((f32[8,8,256]{2,1,0:T(8,128)}), f32[8,8,256]{2,1,0:T(8,128)S(1)}, u32[]{:S(2)}, u32[]{:S(2)}) async-start(f32[8,8,256]{2,1,0:T(8,128)} %bitcast.16), calls=%async_computation.1 | async-start | bytes 131072 | tf_op jit(solution)/shard_map/all_to_all | solution.py:99
  112.8 3.3 %multiply_add_fusion.3 = f32[3,8,8,8,256]{4,3,2,1,0:T(8,128)} fusion(f32[3,8,8,8,256]{4,3,2,1,0:T(8,128)} %bitcast.134, f32[3,8,8,8,256]{4,3,2,1,0:T(8,128)} %scatter-add.55), kind=kLoop, calls=%fused_computation.14 | loop fusion | flops 786432 | bytes 4718592 | tf_op jit(solution)/shard_map/add | solution.py:40
  116.1 2.4 %all-to-all-done = f32[8,8,256]{2,1,0:T(8,128)S(1)} async-done(((f32[8,8,256]{2,1,0:T(8,128)}), f32[8,8,256]{2,1,0:T(8,128)S(1)}, u32[]{:S(2)}, u32[]{:S(2)}) %all-to-all-start) | async-done | bytes 65568 | tf_op jit(solution)/shard_map/all_to_all | solution.py:99
  120.3 2.3 scatter-add.56
  122.7 2.8 %multiply_add_fusion.2 = f32[3,8,8,8,256]{4,3,2,1,0:T(8,128)S(1)} fusion(f32[3,8,8,8,256]{4,3,2,1,0:T(8,128)} %bitcast.129, f32[3,8,8,8,256]{4,3,2,1,0:T(8,128)} %bitcast.132, f32[3,8,8,8,256]{4,3,2,1,0:T(8,128)} %scatter-add.56), kind=kLoop, calls=%fused_computation.13 | loop fusion | flops 1179648 | bytes 6291456 | tf_op jit(solution)/shard_map/add | solution.py:110
  127.3 3.6 %collective-permute-start.11 = (f32[3,1,8,8,256]{4,2,1,0,3:T(8,128)S(1)}, f32[3,1,8,8,256]{4,2,1,0,3:T(8,128)}, u32[]{:S(2)}, u32[]{:S(2)}) collective-permute-start(f32[3,1,8,8,256]{4,2,1,0,3:T(8,128)S(1)} %slice.605), channel_id=1, source_target_pairs={{0,4},{4,8},{8,12},{12,16},{16,20},{20,24},{24,28},{1,5},{5,9},{9,... | collective-permute-start | bytes 589832 | tf_op jit(solution)/shard_map/ppermute | solution.py:17
  132.2 6.5 %fusion.5 = f32[3,512,256]{1,2,0:T(8,128)} fusion(f32[3,512,256]{2,1,0:T(8,128)S(1)} %bitcast.124, f32[1,3,512,512]{3,2,1,0:T(8,128)S(1)} %copy-done), kind=kOutput, calls=%fused_computation.15 | convolution fusion | flops 2415919104 | bytes 6291456 | tf_op jit(solution)/shard_map/dab,dbf->daf/dot_general | solution.py:39
  140.4 3.1 %copy.82 = f32[3,512,256]{2,1,0:T(8,128)} copy(f32[3,512,256]{1,2,0:T(8,128)} %fusion.5) | data formatting | bytes 3145728 | tf_op jit(solution)/shard_map/dab,dbf->daf/dot_general | solution.py:39
  147.1 3.7 %collective-permute-done.18 = f32[64,256]{1,0:T(8,128)S(1)} collective-permute-done((f32[64,256]{1,0:T(8,128)}, f32[64,256]{1,0:T(8,128)S(1)}, u32[]{:S(2)}, u32[]{:S(2)}) %collective-permute-start.18) | collective-permute-done | bytes 65568 | tf_op jit(solution)/shard_map/ppermute | solution.py:82
  150.8 1.9 constant_dynamic-update-slice_fusion.12
  154.0 2.6 %collective-permute-done.19 = f32[64,256]{1,0:T(8,128)S(1)} collective-permute-done((f32[64,256]{1,0:T(8,128)S(1)}, f32[64,256]{1,0:T(8,128)S(1)}, u32[]{:S(2)}, u32[]{:S(2)}) %collective-permute-start.19) | collective-permute-done | bytes 65568 | tf_op jit(solution)/shard_map/ppermute | solution.py:82
  158.7 3.7 %collective-permute-done.20 = f32[64,256]{1,0:T(8,128)S(1)} collective-permute-done((f32[64,256]{1,0:T(8,128)S(1)}, f32[64,256]{1,0:T(8,128)S(1)}, u32[]{:S(2)}, u32[]{:S(2)}) %collective-permute-start.20) | collective-permute-done | bytes 65568 | tf_op jit(solution)/shard_map/ppermute | solution.py:82
  163.5 11.2 %collective-permute-start.13 = (f32[3,10,1,8,256]{4,2,1,0,3:T(1,128)}, f32[3,10,1,8,256]{4,2,1,0,3:T(1,128)}, u32[]{:S(2)}, u32[]{:S(2)}) collective-permute-start(f32[3,10,1,8,256]{4,2,1,0,3:T(1,128)} %get-tuple-element.180), channel_id=1, source_target_pairs={{0,1},{1,2},{2,3},{4,5},{5,6},{6,7},{8,9},{9,10},{10,11},{12,13},{... | collective-permute-start | bytes 737288 | tf_op jit(solution)/shard_map/ppermute | solution.py:17
  174.6 2.2 collective-permute-start.14
  178.8 3.3 %gather_fusion.2 = f32[512,256]{1,0:T(8,128)} fusion(f32[512,256]{1,0:T(8,128)} %fusion.8, s32[1024]{0:T(1024)S(1)} %pad_clamp_fusion.1), kind=kCustom, calls=%fused_computation.2.clone | custom fusion | bytes 1050624 | tf_op jit(solution)/shard_map/jit(_take)/gather | solution.py:86
  182.0 1.9 convolution_bitcast_fusion
  186.5 1.8 fusion.21
  188.3 4.5 %scatter-add.61 = f32[3,8,8,8,256]{4,2,1,0,3:T(8,128)} dynamic-update-slice(f32[3,8,8,8,256]{4,2,1,0,3:T(8,128)} %get-tuple-element.192, f32[3,8,1,8,256]{4,2,1,0,3:T(1,128)S(1)} %fusion.21, s32[]{:T(128)} %constant.415.clone.1, s32[]{:T(128)} %constant.415.clone.1, s32[]{:T(128)} %constant.415.clone.1, s32[]{:T(128)} %constant.415.clone.1, s32[]{:T(128)} %constant.415.clone.1) | dynamic-update-slice | bytes 393220 | tf_op jit(solution)/shard_map/scatter-add | solution.py:32
  192.8 1.9 fusion.20
  194.7 4.5 %scatter-add.64 = f32[3,8,8,8,256]{4,2,1,0,3:T(8,128)} dynamic-update-slice(f32[3,8,8,8,256]{4,2,1,0,3:T(8,128)} %scatter-add.61, f32[3,8,1,8,256]{4,2,1,0,3:T(1,128)S(1)} %fusion.20, s32[]{:T(128)} %constant.415.clone.1, s32[]{:T(128)} %constant.415.clone.1, s32[]{:T(128)} %constant.416.clone.1, s32[]{:T(128)} %constant.415.clone.1, s32[]{:T(128)} %constant.415.clone.1) | dynamic-update-slice | bytes 393220 | tf_op jit(solution)/shard_map/scatter-add | solution.py:33
  199.2 1.8 fusion.19
  202.0 3.5 %copy.90 = f32[3,8,8,8,256]{4,3,2,1,0:T(8,128)} copy(f32[3,8,8,8,256]{4,2,1,0,3:T(8,128)} %fusion.19) | data formatting | bytes 3145728 | tf_op jit(solution)/shard_map/scatter-add | solution.py:37
  207.2 4.0 %scatter-add.66 = f32[3,8,8,8,256]{4,3,2,1,0:T(8,128)} dynamic-update-slice(f32[3,8,8,8,256]{4,3,2,1,0:T(8,128)} %copy.90, f32[2,8,8,1,256]{4,3,2,1,0:T(1,128)S(1)} %fusion.28, s32[]{:T(128)} %constant.417.clone.1, s32[]{:T(128)} %constant.415.clone.1, s32[]{:T(128)} %constant.415.clone.1, s32[]{:T(128)} %constant.415.clone.1, s32[]{:T(128)} %constant.415.clone.1) | dynamic-update-slice | bytes 262148 | tf_op jit(solution)/shard_map/scatter-add | solution.py:38
  212.9 5.7 %all-to-all-start.1 = ((f32[8,8,256]{2,1,0:T(8,128)}), f32[8,8,256]{2,1,0:T(8,128)S(1)}, u32[]{:S(2)}, u32[]{:S(2)}) async-start(f32[8,8,256]{2,1,0:T(8,128)} %bitcast.26), calls=%async_computation.3 | async-start | bytes 131072 | tf_op jit(solution)/shard_map/all_to_all | solution.py:99
  218.6 3.3 %multiply_add_fusion.1 = f32[3,8,8,8,256]{4,3,2,1,0:T(8,128)} fusion(f32[3,8,8,8,256]{4,3,2,1,0:T(8,128)} %bitcast.131, f32[3,8,8,8,256]{4,3,2,1,0:T(8,128)} %scatter-add.66), kind=kLoop, calls=%fused_computation.12 | loop fusion | flops 786432 | bytes 4718592 | tf_op jit(solution)/shard_map/add | solution.py:40
  221.9 2.4 %all-to-all-done.1 = f32[8,8,256]{2,1,0:T(8,128)S(1)} async-done(((f32[8,8,256]{2,1,0:T(8,128)}), f32[8,8,256]{2,1,0:T(8,128)S(1)}, u32[]{:S(2)}, u32[]{:S(2)}) %all-to-all-start.1) | async-done | bytes 65568 | tf_op jit(solution)/shard_map/all_to_all | solution.py:99
  226.2 2.3 scatter-add.69
  228.5 3.9 %multiply_add_fusion = f32[3,8,8,8,256]{4,3,2,1,0:T(8,128)} fusion(f32[3,8,8,8,256]{4,3,2,1,0:T(8,128)} %copy-done.1, f32[3,8,8,8,256]{4,3,2,1,0:T(8,128)} %bitcast.133, f32[3,8,8,8,256]{4,3,2,1,0:T(8,128)} %scatter-add.69), kind=kLoop, calls=%fused_computation.11 | loop fusion | flops 1179648 | bytes 6291456 | tf_op jit(solution)/shard_map/add | solution.py:110
  (122 shorter events, 51.2 us)
Async XLA Ops:
  7.2 9.3 %copy-start = (f32[1,3,512,512]{3,2,1,0:T(8,128)S(1)}, f32[1,3,512,512]{3,2,1,0:T(8,128)}, u32[]{:S(2)}) copy-start(f32[1,3,512,512]{3,2,1,0:T(8,128)} %param.39) | copy-start | bytes 9437188
  7.2 98.1 %reduce-scatter.3.cloned.1.call-start = ((), (), s32[]{:S(2)}) async-start(), calls=%async_computation.4 | async-start | bytes 327680 | tf_op jit(solution)/shard_map/reduce_scatter | solution.py:90
  7.2 8.6 %copy-start.2 = (f32[1,3,512,256]{3,2,1,0:T(8,128)S(1)}, f32[1,3,512,256]{3,2,1,0:T(8,128)}, u32[]{:S(2)}) copy-start(f32[1,3,512,256]{3,2,1,0:T(8,128)} %param.41) | copy-start | bytes 4718596
  7.2 9.3 %copy-start.8 = (s32[1,512]{1,0:T(1,128)S(1)}, s32[1,512]{1,0:T(1,128)}, u32[]{:S(2)}) copy-start(s32[1,512]{1,0:T(1,128)} %param.43) | copy-start | bytes 6148
  9.3 1.2 copy-start.3
  11.2 32.0 %collective-permute-start = (f32[3,1,8,8,256]{4,2,1,0,3:T(8,128)}, f32[3,1,8,8,256]{4,2,1,0,3:T(8,128)}, u32[]{:S(2)}, u32[]{:S(2)}) collective-permute-start(f32[3,1,8,8,256]{4,2,1,0,3:T(8,128)} %slice.588), channel_id=1, source_target_pairs={{0,4},{4,8},{8,12},{12,16},{16,20},{20,24},{24,28},{1,5},{5,9},{9,... | collective-permute-start | bytes 589832 | tf_op jit(solution)/shard_map/ppermute | solution.py:17
  15.8 9.5 %collective-permute-start.4 = (f32[64,256]{1,0:T(8,128)S(1)}, f32[64,256]{1,0:T(8,128)S(1)}, u32[]{:S(2)}, u32[]{:S(2)}) collective-permute-start(f32[64,256]{1,0:T(8,128)S(1)} %bitcast.141), channel_id=1, source_target_pairs={{0,4},{4,8},{8,12},{12,16},{16,20},{20,24},{24,28},{28,0},{1,5},{5... | collective-permute-start | bytes 196616 | tf_op jit(solution)/shard_map/ppermute | solution.py:82
  25.3 18.9 %copy-start.6 = (f32[64,256]{1,0:T(8,128)}, f32[64,256]{1,0:T(8,128)S(1)}, u32[]{:S(2)}) copy-start(f32[64,256]{1,0:T(8,128)S(1)} %collective-permute-done.4) | copy-start | bytes 196612
  25.3 6.0 %collective-permute-start.5 = (f32[64,256]{1,0:T(8,128)S(1)}, f32[64,256]{1,0:T(8,128)}, u32[]{:S(2)}, u32[]{:S(2)}) collective-permute-start(f32[64,256]{1,0:T(8,128)S(1)} %collective-permute-done.4), channel_id=1, source_target_pairs={{0,4},{4,8},{8,12},{12,16},{16,20},{20,24},{24,28},{28,0},{1,5},{5... | collective-permute-start | bytes 196616 | tf_op jit(solution)/shard_map/ppermute | solution.py:82
  31.3 6.0 %collective-permute-start.6 = (f32[64,256]{1,0:T(8,128)}, f32[64,256]{1,0:T(8,128)S(1)}, u32[]{:S(2)}, u32[]{:S(2)}) collective-permute-start(f32[64,256]{1,0:T(8,128)} %collective-permute-done.5), channel_id=1, source_target_pairs={{0,4},{4,8},{8,12},{12,16},{16,20},{20,24},{24,28},{28,0},{1,5},{5... | collective-permute-start | bytes 196616 | tf_op jit(solution)/shard_map/ppermute | solution.py:82
  37.3 5.8 %collective-permute-start.7 = (f32[64,256]{1,0:T(8,128)S(1)}, f32[64,256]{1,0:T(8,128)S(1)}, u32[]{:S(2)}, u32[]{:S(2)}) collective-permute-start(f32[64,256]{1,0:T(8,128)S(1)} %collective-permute-done.6), channel_id=1, source_target_pairs={{0,4},{4,8},{8,12},{12,16},{16,20},{20,24},{24,28},{28,0},{1,5},{5... | collective-permute-start | bytes 196616 | tf_op jit(solution)/shard_map/ppermute | solution.py:82
  43.1 5.9 %collective-permute-start.8 = (f32[64,256]{1,0:T(8,128)S(1)}, f32[64,256]{1,0:T(8,128)S(1)}, u32[]{:S(2)}, u32[]{:S(2)}) collective-permute-start(f32[64,256]{1,0:T(8,128)S(1)} %collective-permute-done.7), channel_id=1, source_target_pairs={{0,4},{4,8},{8,12},{12,16},{16,20},{20,24},{24,28},{28,0},{1,5},{5... | collective-permute-start | bytes 196616 | tf_op jit(solution)/shard_map/ppermute | solution.py:82
  44.2 10.7 %collective-permute-start.1 = (f32[3,1,8,8,256]{4,2,1,0,3:T(8,128)S(1)}, f32[3,1,8,8,256]{4,2,1,0,3:T(8,128)S(1)}, u32[]{:S(2)}, u32[]{:S(2)}) collective-permute-start(f32[3,1,8,8,256]{4,2,1,0,3:T(8,128)S(1)} %get-tuple-element.187), channel_id=1, source_target_pairs={{4,0},{8,4},{12,8},{16,12},{20,16},{24,20},{28,24},{5,1},{9,5},{13... | collective-permute-start | bytes 589832 | tf_op jit(solution)/shard_map/ppermute | solution.py:20
  49.0 5.9 %collective-permute-start.9 = (f32[64,256]{1,0:T(8,128)S(1)}, f32[64,256]{1,0:T(8,128)S(1)}, u32[]{:S(2)}, u32[]{:S(2)}) collective-permute-start(f32[64,256]{1,0:T(8,128)S(1)} %collective-permute-done.8), channel_id=1, source_target_pairs={{0,4},{4,8},{8,12},{12,16},{16,20},{20,24},{24,28},{28,0},{1,5},{5... | collective-permute-start | bytes 196616 | tf_op jit(solution)/shard_map/ppermute | solution.py:82
  52.2 18.8 %copy-start.7 = (f32[64,256]{1,0:T(8,128)S(1)}, f32[64,256]{1,0:T(8,128)}, u32[]{:S(2)}) copy-start(f32[64,256]{1,0:T(8,128)} %copy-done.6) | copy-start | bytes 196612
  54.9 15.1 %collective-permute-start.10 = (f32[64,256]{1,0:T(8,128)S(1)}, f32[64,256]{1,0:T(8,128)S(1)}, u32[]{:S(2)}, u32[]{:S(2)}) collective-permute-start(f32[64,256]{1,0:T(8,128)S(1)} %collective-permute-done.9), channel_id=1, source_target_pairs={{0,4},{4,8},{8,12},{12,16},{16,20},{20,24},{24,28},{28,0},{1,5},{5... | collective-permute-start | bytes 196616 | tf_op jit(solution)/shard_map/ppermute | solution.py:82
  57.7 22.0 %collective-permute-start.2 = (f32[3,10,1,8,256]{4,2,1,0,3:T(1,128)}, f32[3,10,1,8,256]{4,2,1,0,3:T(1,128)}, u32[]{:S(2)}, u32[]{:S(2)}) collective-permute-start(f32[3,10,1,8,256]{4,2,1,0,3:T(1,128)} %get-tuple-element.182), channel_id=1, source_target_pairs={{0,1},{1,2},{2,3},{4,5},{5,6},{6,7},{8,9},{9,10},{10,11},{12,13},{... | collective-permute-start | bytes 737288 | tf_op jit(solution)/shard_map/ppermute | solution.py:17
  67.9 18.6 %collective-permute-start.3 = (f32[3,10,1,8,256]{4,2,1,0,3:T(1,128)}, f32[3,10,1,8,256]{4,2,1,0,3:T(1,128)}, u32[]{:S(2)}, u32[]{:S(2)}) collective-permute-start(f32[3,10,1,8,256]{4,2,1,0,3:T(1,128)} %get-tuple-element.181), channel_id=1, source_target_pairs={{1,0},{2,1},{3,2},{5,4},{6,5},{7,6},{9,8},{10,9},{11,10},{13,12},{... | collective-permute-start | bytes 737288 | tf_op jit(solution)/shard_map/ppermute | solution.py:20
  107.0 11.5 %all-to-all-start = ((f32[8,8,256]{2,1,0:T(8,128)}), f32[8,8,256]{2,1,0:T(8,128)S(1)}, u32[]{:S(2)}, u32[]{:S(2)}) async-start(f32[8,8,256]{2,1,0:T(8,128)} %bitcast.16), calls=%async_computation.1 | async-start | bytes 131072 | tf_op jit(solution)/shard_map/all_to_all | solution.py:99
  112.7 98.5 %reduce-scatter.5.cloned.1.call-start = ((), (), s32[]{:S(2)}) async-start(), calls=%async_computation.5 | async-start | bytes 327680 | tf_op jit(solution)/shard_map/reduce_scatter | solution.py:90
  125.4 14.2 %copy-start.1 = (f32[3,8,8,8,256]{4,3,2,1,0:T(8,128)}, f32[3,8,8,8,256]{4,3,2,1,0:T(8,128)S(1)}, u32[]{:S(2)}) copy-start(f32[3,8,8,8,256]{4,3,2,1,0:T(8,128)S(1)} %multiply_add_fusion.2) | copy-start | bytes 4718596
  125.5 6.7 %collective-permute-start.15 = (f32[64,256]{1,0:T(8,128)S(1)}, f32[64,256]{1,0:T(8,128)S(1)}, u32[]{:S(2)}, u32[]{:S(2)}) collective-permute-start(f32[64,256]{1,0:T(8,128)S(1)} %bitcast.142), channel_id=1, source_target_pairs={{0,4},{4,8},{8,12},{12,16},{16,20},{20,24},{24,28},{28,0},{1,5},{5... | collective-permute-start | bytes 196616 | tf_op jit(solution)/shard_map/ppermute | solution.py:82
  126.2 1.1 copy-start.4
  127.3 17.3 %collective-permute-start.11 = (f32[3,1,8,8,256]{4,2,1,0,3:T(8,128)S(1)}, f32[3,1,8,8,256]{4,2,1,0,3:T(8,128)}, u32[]{:S(2)}, u32[]{:S(2)}) collective-permute-start(f32[3,1,8,8,256]{4,2,1,0,3:T(8,128)S(1)} %slice.605), channel_id=1, source_target_pairs={{0,4},{4,8},{8,12},{12,16},{16,20},{20,24},{24,28},{1,5},{5,9},{9,... | collective-permute-start | bytes 589832 | tf_op jit(solution)/shard_map/ppermute | solution.py:17
  132.2 6.5 %collective-permute-start.16 = (f32[64,256]{1,0:T(8,128)S(1)}, f32[64,256]{1,0:T(8,128)S(1)}, u32[]{:S(2)}, u32[]{:S(2)}) collective-permute-start(f32[64,256]{1,0:T(8,128)S(1)} %collective-permute-done.15), channel_id=1, source_target_pairs={{0,4},{4,8},{8,12},{12,16},{16,20},{20,24},{24,28},{28,0},{1,5},{5... | collective-permute-start | bytes 196616 | tf_op jit(solution)/shard_map/ppermute | solution.py:82
  138.7 5.9 %collective-permute-start.17 = (f32[64,256]{1,0:T(8,128)S(1)}, f32[64,256]{1,0:T(8,128)}, u32[]{:S(2)}, u32[]{:S(2)}) collective-permute-start(f32[64,256]{1,0:T(8,128)S(1)} %collective-permute-done.16), channel_id=1, source_target_pairs={{0,4},{4,8},{8,12},{12,16},{16,20},{20,24},{24,28},{28,0},{1,5},{5... | collective-permute-start | bytes 196616 | tf_op jit(solution)/shard_map/ppermute | solution.py:82
  144.7 6.1 %collective-permute-start.18 = (f32[64,256]{1,0:T(8,128)}, f32[64,256]{1,0:T(8,128)S(1)}, u32[]{:S(2)}, u32[]{:S(2)}) collective-permute-start(f32[64,256]{1,0:T(8,128)} %collective-permute-done.17), channel_id=1, source_target_pairs={{0,4},{4,8},{8,12},{12,16},{16,20},{20,24},{24,28},{28,0},{1,5},{5... | collective-permute-start | bytes 196616 | tf_op jit(solution)/shard_map/ppermute | solution.py:82
  145.8 11.3 %collective-permute-start.12 = (f32[3,1,8,8,256]{4,2,1,0,3:T(8,128)S(1)}, f32[3,1,8,8,256]{4,2,1,0,3:T(8,128)S(1)}, u32[]{:S(2)}, u32[]{:S(2)}) collective-permute-start(f32[3,1,8,8,256]{4,2,1,0,3:T(8,128)S(1)} %get-tuple-element.185), channel_id=1, source_target_pairs={{4,0},{8,4},{12,8},{16,12},{20,16},{24,20},{28,24},{5,1},{9,5},{13... | collective-permute-start | bytes 589832 | tf_op jit(solution)/shard_map/ppermute | solution.py:20
  150.8 5.8 %collective-permute-start.19 = (f32[64,256]{1,0:T(8,128)S(1)}, f32[64,256]{1,0:T(8,128)S(1)}, u32[]{:S(2)}, u32[]{:S(2)}) collective-permute-start(f32[64,256]{1,0:T(8,128)S(1)} %collective-permute-done.18), channel_id=1, source_target_pairs={{0,4},{4,8},{8,12},{12,16},{16,20},{20,24},{24,28},{28,0},{1,5},{5... | collective-permute-start | bytes 196616 | tf_op jit(solution)/shard_map/ppermute | solution.py:82
  156.6 5.8 %collective-permute-start.20 = (f32[64,256]{1,0:T(8,128)S(1)}, f32[64,256]{1,0:T(8,128)S(1)}, u32[]{:S(2)}, u32[]{:S(2)}) collective-permute-start(f32[64,256]{1,0:T(8,128)S(1)} %collective-permute-done.19), channel_id=1, source_target_pairs={{0,4},{4,8},{8,12},{12,16},{16,20},{20,24},{24,28},{28,0},{1,5},{5... | collective-permute-start | bytes 196616 | tf_op jit(solution)/shard_map/ppermute | solution.py:82
  162.4 14.4 %collective-permute-start.21 = (f32[64,256]{1,0:T(8,128)S(1)}, f32[64,256]{1,0:T(8,128)S(1)}, u32[]{:S(2)}, u32[]{:S(2)}) collective-permute-start(f32[64,256]{1,0:T(8,128)S(1)} %collective-permute-done.20), channel_id=1, source_target_pairs={{0,4},{4,8},{8,12},{12,16},{16,20},{20,24},{24,28},{28,0},{1,5},{5... | collective-permute-start | bytes 196616 | tf_op jit(solution)/shard_map/ppermute | solution.py:82
  163.5 23.0 %collective-permute-start.13 = (f32[3,10,1,8,256]{4,2,1,0,3:T(1,128)}, f32[3,10,1,8,256]{4,2,1,0,3:T(1,128)}, u32[]{:S(2)}, u32[]{:S(2)}) collective-permute-start(f32[3,10,1,8,256]{4,2,1,0,3:T(1,128)} %get-tuple-element.180), channel_id=1, source_target_pairs={{0,1},{1,2},{2,3},{4,5},{5,6},{6,7},{8,9},{9,10},{10,11},{12,13},{... | collective-permute-start | bytes 737288 | tf_op jit(solution)/shard_map/ppermute | solution.py:17
  174.6 18.2 %collective-permute-start.14 = (f32[3,10,1,8,256]{4,2,1,0,3:T(1,128)}, f32[3,10,1,8,256]{4,2,1,0,3:T(1,128)}, u32[]{:S(2)}, u32[]{:S(2)}) collective-permute-start(f32[3,10,1,8,256]{4,2,1,0,3:T(1,128)} %get-tuple-element.179), channel_id=1, source_target_pairs={{1,0},{2,1},{3,2},{5,4},{6,5},{7,6},{9,8},{10,9},{11,10},{13,12},{... | collective-permute-start | bytes 737288 | tf_op jit(solution)/shard_map/ppermute | solution.py:20
  184.7 8.1 %copy-start.5 = (f32[3,8,1,8,256]{4,3,2,1,0:T(8,128)S(1)}, f32[3,8,1,8,256]{4,3,2,1,0:T(8,128)}, u32[]{:S(2)}) copy-start(f32[3,8,1,8,256]{4,3,2,1,0:T(8,128)} %get-tuple-element.183) | copy-start | bytes 589828
  212.9 11.5 %all-to-all-start.1 = ((f32[8,8,256]{2,1,0:T(8,128)}), f32[8,8,256]{2,1,0:T(8,128)S(1)}, u32[]{:S(2)}, u32[]{:S(2)}) async-start(f32[8,8,256]{2,1,0:T(8,128)} %bitcast.26), calls=%async_computation.3 | async-start | bytes 131072 | tf_op jit(solution)/shard_map/all_to_all | solution.py:99
Sparse Core Ops, SparseCore 0:
  79.8 21.2 reduce-scatter.2
  186.6 21.2 reduce-scatter.4
